TPU v7x, 512 devices: a whole 4x8x8 slice. The times are simulated.
512 devices in a mesh: row: 32 (over z_lo, x, core), col: 16 (over z_hi, y).
Axes of the slice: x: 4, y: 8, z: 8 (z_hi: 2, z_lo: 4; z = z_hi * 4 + z_lo), core: 2. Of those that a mesh axis runs over, the one named last changes fastest.
Arguments:
- state: float32 [32, 2, 16, 256, 256], P('row', None, 'col'), may hold values from -6 to 6
- a_tiles: float32 [32, 2, 16, 256, 256], P('row', None, 'col'), may hold values from -0.375 to 0.375
- inverses: float32 [32, 256, 256], P('row'), may hold values from -0.225 to 1.025
Outputs:
- state_out: float32 [32, 2, 16, 256, 256], P('row', None, 'col')
All inputs are finite; a program needn't handle non-finite values.
Results may differ from a plain program's by a relative error of at most 0.0001.
Values sent between devices are 32-bit elements; how exact they have to be, the bound alone decides.
A program may use at most 64 MiB of HBM per device.

v0:
```python
import jax
import jax.numpy as jnp
from jax import lax
from jax.sharding import PartitionSpec as P

FRONTS = 3
DOUBLINGS = 5
HIGH = lax.Precision.HIGHEST
shift_half = 0.5


def swapped(value, axis, stride):
    mask = 2**stride
    pairs = [(source, source ^ mask) for source in range(lax.axis_size(axis))]
    return lax.ppermute(value, axis, pairs)


def passed_along(block, axis, distance):
    devices = range(lax.axis_size(axis))
    route = [((i - distance) % len(devices), i) for i in devices]
    return lax.ppermute(block, axis, route)


def spread(value, axis, source):
    kept = jnp.where(lax.axis_index(axis) == source, value, 0).astype(value.dtype)
    return lax.psum(kept, axis)


def product(left, right):
    return jnp.dot(left, right, precision=HIGH, preferred_element_type=jnp.float32)


def product_transposed(left, right):
    return lax.dot_general(
        left, right, (((1,), (1,)), ((), ())), precision=HIGH, preferred_element_type=jnp.float32
    )


def batched_product(left, right):
    return jnp.einsum(
        "nab,nbc->nac", left, right, precision=HIGH, preferred_element_type=jnp.float32
    )


def across_cols(pieces):
    return lax.all_to_all(pieces, "col", split_axis=1, concat_axis=1, tiled=True)


def mirrored(tile_set):
    slot_count = tile_set.shape[0]
    tile_order = tile_set.shape[1]
    col_count = lax.axis_size("col")
    slab_rows = tile_order // col_count
    section_one = across_cols(tile_set.reshape(slot_count, col_count, slab_rows, tile_order))
    by_target = section_one.reshape(slot_count * col_count, slab_rows, tile_order)
    section_two = lax.all_to_all(by_target, "row", split_axis=0, concat_axis=0, tiled=True)
    section_three = across_cols(section_two.reshape(slot_count, col_count, slab_rows, tile_order))
    return section_three.reshape(slot_count, tile_order, tile_order)


def flipped(tile_set, col_count):
    levels = col_count.bit_length() - 1
    for bit_pos in range(levels):
        tile_set = swapped(tile_set, "col", bit_pos)
    return tile_set


def per_device(state, a_tiles, inverses):
    slot_count = state.shape[1]
    tile_order = state.shape[3]
    col_count = lax.axis_size("col")
    height = lax.axis_size("row")
    row_here = lax.axis_index("row")
    col_here = lax.axis_index("col")
    current = state.reshape(slot_count, tile_order, tile_order)
    coupling = a_tiles.reshape(slot_count, tile_order, tile_order)
    own_inverse = inverses.reshape(tile_order, tile_order)
    identity_tile = jnp.eye(tile_order, dtype=jnp.float32)
    left_powers = [identity_tile - shift_half * own_inverse]
    for level in range(DOUBLINGS - 1):
        left_powers.append(product(left_powers[-1], left_powers[-1]))
    column_inverse = mirrored(jnp.broadcast_to(own_inverse, (slot_count, tile_order, tile_order)))
    right_list = [identity_tile[None] - shift_half * column_inverse]
    for level in range(DOUBLINGS - 1):
        right_list.append(batched_product(right_list[-1], right_list[-1]))
    right_powers = jnp.stack(right_list)
    tile_cols = jnp.arange(slot_count, dtype=jnp.int32) * col_count + col_here
    tile_sum = row_here + tile_cols
    for front_step in range(FRONTS):
        front_sum = height - 1 - front_step
        source_a = flipped(coupling, col_count)
        if front_step > 0:
            source_a = passed_along(source_a, "col", -front_step)
        front_col = front_sum - row_here
        front_slot = jnp.clip(front_col // col_count, 0, slot_count - 1)
        own_tile = lax.dynamic_index_in_dim(current, front_slot, 0, keepdims=False)
        mirror = mirrored(current)
        far_tile = lax.dynamic_index_in_dim(mirror, front_slot, 0, keepdims=False)
        right_side = own_tile + far_tile.T
        right_inverse = lax.dynamic_index_in_dim(column_inverse, front_slot, 0, keepdims=False)
        powers_here = lax.dynamic_index_in_dim(right_powers, front_slot, 1, keepdims=False)
        solution = shift_half * product_transposed(product(own_inverse, right_side), right_inverse)
        for level in range(DOUBLINGS):
            solution = solution + product_transposed(
                product(left_powers[level], solution), powers_here[level]
            )
        passed = []
        for slot_pos in range(slot_count):
            root_row = jnp.clip(front_sum - tile_cols[slot_pos], 0, height - 1)
            passed.append(spread(solution, "row", root_row))
        below_rows = front_sum - tile_cols
        a_slot = jnp.clip(below_rows // col_count, 0, slot_count - 1)
        a_pick = jnp.take(source_a, a_slot, axis=0)
        update = batched_product(a_pick, jnp.stack(passed))
        shrink = (tile_sum < front_sum)[:, None, None]
        place = (tile_sum == front_sum)[:, None, None]
        current = jnp.where(shrink, current - update, jnp.where(place, solution[None], current))
    return current.reshape(state.shape)


def solution(mesh):
    in_specs = (
        P("row", None, "col", None, None),
        P("row", None, "col", None, None),
        P("row", None, None),
    )
    out_specs = P("row", None, "col", None, None)
    return jax.shard_map(
        per_device, mesh=mesh, in_specs=in_specs, out_specs=out_specs, check_vma=False
    )
```

profile of v0, /device:TPU:1, one launch (start us, length us, event | category | flops | bytes accessed | tf_op | source)
XLA Modules:
  0.0 1221.0 jit_solution(3985047102242037960)
XLA Ops:
  6.5 1.1 copy.25
  7.6 34.1 %all_to_all.60 = f32[2,16,16,256]{3,2,0,1:T(8,128)S(1)} all-to-all(f32[2,16,16,256]{3,2,0,1:T(8,128)S(1)} %copy.25), channel_id=1, replica_groups=mesh['row'=32,'col'=16] {'col'}, dimensions={1} | all-to-all | bytes 1048576 | tf_op jit(solution)/shard_map/all_to_all | solution.py:46
  41.7 1.8 broadcast_in_dim.91
  43.5 5.7 all-to-all-start.3
  49.2 0.8 copy.26
  50.0 16.1 %all-to-all-done.3 = f32[2,16,16,256]{3,2,0,1:T(8,128)S(1)} async-done(((f32[2,16,16,256]{3,2,0,1:T(8,128)}), f32[2,16,16,256]{3,2,0,1:T(8,128)S(1)}, u32[]{:S(2)}, u32[]{:S(2)}) %all-to-all-start.3) | async-done | bytes 524320 | tf_op jit(solution)/shard_map/all_to_all | solution.py:46
  66.1 10.6 all-to-all-start.1
  76.8 0.8 copy.30
  77.6 15.6 %all-to-all-done.1 = f32[32,16,256]{2,1,0:T(8,128)S(1)} async-done(((f32[32,16,256]{2,1,0:T(8,128)}), f32[32,16,256]{2,1,0:T(8,128)S(1)}, u32[]{:S(2)}, u32[]{:S(2)}) %all-to-all-start.1) | async-done | bytes 524320 | tf_op jit(solution)/shard_map/all_to_all | solution.py:56
  93.2 4.1 all-to-all-start.4
  97.3 3.2 collective-permute-start
  100.5 0.8 copy.27
  101.4 12.4 %all-to-all-done.4 = f32[32,16,256]{2,1,0:T(8,128)S(1)} async-done(((f32[32,16,256]{2,1,0:T(8,128)}), f32[32,16,256]{2,1,0:T(8,128)S(1)}, u32[]{:S(2)}, u32[]{:S(2)}) %all-to-all-start.4) | async-done | bytes 524320 | tf_op jit(solution)/shard_map/all_to_all | solution.py:56
  113.7 4.5 all-to-all-start.2
  118.7 4.2 collective-permute-start.1
  123.3 0.8 copy.31
  124.1 13.2 %all-to-all-done.2 = f32[2,16,16,256]{3,2,0,1:T(8,128)S(1)} async-done(((f32[2,16,16,256]{3,2,0,1:T(8,128)}), f32[2,16,16,256]{3,2,0,1:T(8,128)S(1)}, u32[]{:S(2)}, u32[]{:S(2)}) %all-to-all-start.2) | async-done | bytes 524320 | tf_op jit(solution)/shard_map/all_to_all | solution.py:46
  137.4 5.7 all-to-all-start.5
  143.1 0.6 fusion.92
  143.8 15.3 %collective-permute-done.1 = f32[2,256,256]{2,1,0:T(8,128)} collective-permute-done((f32[2,256,256]{2,1,0:T(8,128)}, f32[2,256,256]{2,1,0:T(8,128)}, u32[]{:S(2)}, u32[]{:S(2)}) %collective-permute-start.1) | collective-permute-done | bytes 524320 | tf_op jit(solution)/shard_map/ppermute | solution.py:15
  159.0 8.0 collective-permute-start.2
  169.1 20.2 %collective-permute-done.2 = f32[2,256,256]{2,1,0:T(8,128)} collective-permute-done((f32[2,256,256]{2,1,0:T(8,128)}, f32[2,256,256]{2,1,0:T(8,128)}, u32[]{:S(2)}, u32[]{:S(2)}) %collective-permute-start.2) | collective-permute-done | bytes 524320 | tf_op jit(solution)/shard_map/ppermute | solution.py:15
  189.3 2.1 collective-permute-start.3
  191.6 0.6 fusion.20
  192.2 0.6 convolution_multiply_fusion.2
  193.4 0.7 bitcast_dynamic-update-slice_fusion.2
  194.1 0.7 bitcast_dynamic-update-slice_fusion.1
  194.8 0.7 bitcast_dynamic-update-slice_fusion
  195.5 0.7 fusion.4
  197.8 0.4 convolution_add_fusion.12
  199.4 0.4 convolution_add_fusion.10
  199.8 0.8 select_bitcast_fusion.5
  200.8 11.9 collective-permute-done.3
  212.7 2.4 gather_fusion
  215.1 269.7 %all-reduce.11.cloned.1.call-done = (f32[1,256,256]{2,1,0:T(8,128)}, f32[1,256,256]{2,1,0:T(8,128)}) async-done(((f32[1,256,256]{2,1,0:T(8,128)}, f32[1,256,256]{2,1,0:T(8,128)}), (f32[1,256,256]{2,1,0:T(8,128)}, f32[1,256,256]{2,1,0:T(8,128)})) %all-reduce.11.cloned.1.call-update) | async-done | bytes 524304 | tf_op jit(solution)/shard_map/psum | solution.py:26
  484.8 1.9 fusion.3
  486.7 26.0 %all_to_all.61 = f32[2,16,16,256]{3,2,0,1:T(8,128)S(1)} all-to-all(f32[2,16,16,256]{3,2,0,1:T(8,128)S(1)} %copy.34), channel_id=1, replica_groups=mesh['row'=32,'col'=16] {'col'}, dimensions={1} | all-to-all | bytes 1048576 | tf_op jit(solution)/shard_map/all_to_all | solution.py:46
  512.8 23.9 %all_to_all.62 = f32[32,16,256]{2,1,0:T(8,128)S(1)} all-to-all(f32[32,16,256]{2,1,0:T(8,128)S(1)} %bitcast.223), channel_id=1, replica_groups=mesh['row'=32,'col'=16] {'row'}, dimensions={0} | all-to-all | bytes 1048576 | tf_op jit(solution)/shard_map/all_to_all | solution.py:56
  536.7 0.8 copy.36
  537.5 4.9 all-to-all-start.8
  543.8 9.5 collective-permute-start.4
  553.3 8.2 all-to-all-done.8
  561.7 0.6 fusion.25
  562.4 0.6 convolution_multiply_fusion.1
  565.1 0.4 convolution_add_fusion.7
  566.7 0.4 convolution_add_fusion.5
  567.2 0.8 select_bitcast_fusion.3
  568.1 9.1 collective-permute-done.4
  577.1 2.4 gather_fusion.1
  579.5 270.4 %all-reduce.9.cloned.1.call-done = (f32[1,256,256]{2,1,0:T(8,128)}, f32[1,256,256]{2,1,0:T(8,128)}) async-done(((f32[1,256,256]{2,1,0:T(8,128)}, f32[1,256,256]{2,1,0:T(8,128)}), (f32[1,256,256]{2,1,0:T(8,128)}, f32[1,256,256]{2,1,0:T(8,128)})) %all-reduce.9.cloned.1.call-update) | async-done | bytes 524304 | tf_op jit(solution)/shard_map/psum | solution.py:26
  850.0 1.9 fusion.2
  851.9 26.0 %all_to_all.63 = f32[2,16,16,256]{3,2,0,1:T(8,128)S(1)} all-to-all(f32[2,16,16,256]{3,2,0,1:T(8,128)S(1)} %copy.39), channel_id=1, replica_groups=mesh['row'=32,'col'=16] {'col'}, dimensions={1} | all-to-all | bytes 1048576 | tf_op jit(solution)/shard_map/all_to_all | solution.py:46
  878.0 23.9 %all_to_all.64 = f32[32,16,256]{2,1,0:T(8,128)S(1)} all-to-all(f32[32,16,256]{2,1,0:T(8,128)S(1)} %bitcast.225), channel_id=1, replica_groups=mesh['row'=32,'col'=16] {'row'}, dimensions={0} | all-to-all | bytes 1048576 | tf_op jit(solution)/shard_map/all_to_all | solution.py:56
  901.9 0.8 copy.41
  902.8 4.9 all-to-all-start.11
  909.0 10.5 collective-permute-start.5
  919.4 7.3 all-to-all-done.11
  927.0 0.6 fusion.22
  927.6 0.6 convolution_multiply_fusion
  932.4 0.8 select_bitcast_fusion.1
  933.3 11.4 collective-permute-done.5
  944.7 0.6 gather_fusion.2
  945.3 266.6 %all-reduce.7.cloned.1.call-done = (f32[1,256,256]{2,1,0:T(8,128)}, f32[1,256,256]{2,1,0:T(8,128)}) async-done(((f32[1,256,256]{2,1,0:T(8,128)}, f32[1,256,256]{2,1,0:T(8,128)}), (f32[1,256,256]{2,1,0:T(8,128)}, f32[1,256,256]{2,1,0:T(8,128)})) %all-reduce.7.cloned.1.call-update) | async-done | bytes 524304 | tf_op jit(solution)/shard_map/psum | solution.py:26
  1211.9 2.5 fusion.1
  (80 shorter events, 13.4 us)
Async XLA Ops:
  43.5 53.8 %copy-start.5 = (f32[1,2,1,256,256]{4,3,2,1,0:T(8,128)S(1)}, f32[1,2,1,256,256]{4,3,2,1,0:T(8,128)}, u32[]{:S(2)}) copy-start(f32[1,2,1,256,256]{4,3,2,1,0:T(8,128)} %param.6) | copy-start | bytes 1572868
  43.5 22.6 %all-to-all-start.3 = ((f32[2,16,16,256]{3,2,0,1:T(8,128)}), f32[2,16,16,256]{3,2,0,1:T(8,128)S(1)}, u32[]{:S(2)}, u32[]{:S(2)}) async-start(f32[2,16,16,256]{3,2,0,1:T(8,128)} %broadcast_in_dim.91), calls=%async_computation.3 | async-start | bytes 1048576 | tf_op jit(solution)/shard_map/all_to_all | solution.py:46
  66.1 52.2 %copy-start = (f32[1,256,256]{2,1,0:T(8,128)S(1)}, f32[1,256,256]{2,1,0:T(8,128)}, u32[]{:S(2)}) copy-start(f32[1,256,256]{2,1,0:T(8,128)} %param.7) | copy-start | bytes 786436
  66.1 27.1 %all-to-all-start.1 = ((f32[32,16,256]{2,1,0:T(8,128)}), f32[32,16,256]{2,1,0:T(8,128)S(1)}, u32[]{:S(2)}, u32[]{:S(2)}) async-start(f32[32,16,256]{2,1,0:T(8,128)} %bitcast.5), calls=%async_computation.1 | async-start | bytes 1048576 | tf_op jit(solution)/shard_map/all_to_all | solution.py:56
  93.2 20.6 %all-to-all-start.4 = ((f32[32,16,256]{2,1,0:T(8,128)}), f32[32,16,256]{2,1,0:T(8,128)S(1)}, u32[]{:S(2)}, u32[]{:S(2)}) async-start(f32[32,16,256]{2,1,0:T(8,128)} %bitcast.12), calls=%async_computation.4 | async-start | bytes 1048576 | tf_op jit(solution)/shard_map/all_to_all | solution.py:56
  97.3 21.4 %collective-permute-start = (f32[2,256,256]{2,1,0:T(8,128)S(1)}, f32[2,256,256]{2,1,0:T(8,128)}, u32[]{:S(2)}, u32[]{:S(2)}) collective-permute-start(f32[2,256,256]{2,1,0:T(8,128)S(1)} %bitcast.230), channel_id=1, source_target_pairs={{0,1},{1,0},{2,3},{3,2},{4,5},{5,4},{6,7},{7,6},{8,9},{9,8},{10,11... | collective-permute-start | bytes 1572872 | tf_op jit(solution)/shard_map/ppermute | solution.py:15
  113.7 23.6 %all-to-all-start.2 = ((f32[2,16,16,256]{3,2,0,1:T(8,128)}), f32[2,16,16,256]{3,2,0,1:T(8,128)S(1)}, u32[]{:S(2)}, u32[]{:S(2)}) async-start(f32[2,16,16,256]{3,2,0,1:T(8,128)} %copy.27), calls=%async_computation.2 | async-start | bytes 1048576 | tf_op jit(solution)/shard_map/all_to_all | solution.py:46
  118.7 40.3 %collective-permute-start.1 = (f32[2,256,256]{2,1,0:T(8,128)}, f32[2,256,256]{2,1,0:T(8,128)}, u32[]{:S(2)}, u32[]{:S(2)}) collective-permute-start(f32[2,256,256]{2,1,0:T(8,128)} %collective-permute-done), channel_id=1, source_target_pairs={{0,2},{1,3},{2,0},{3,1},{4,6},{5,7},{6,4},{7,5},{8,10},{9,11},{10,... | collective-permute-start | bytes 1572872 | tf_op jit(solution)/shard_map/ppermute | solution.py:15
  124.1 67.4 %copy-start.4 = (f32[1,2,1,256,256]{4,3,2,1,0:T(8,128)S(1)}, f32[1,2,1,256,256]{4,3,2,1,0:T(8,128)}, u32[]{:S(2)}) copy-start(f32[1,2,1,256,256]{4,3,2,1,0:T(8,128)} %param.5) | copy-start | bytes 1572868
  137.4 54.8 %all-to-all-start.5 = ((f32[2,16,16,256]{3,2,0,1:T(8,128)}), f32[2,16,16,256]{3,2,0,1:T(8,128)S(1)}, u32[]{:S(2)}, u32[]{:S(2)}) async-start(f32[2,16,16,256]{3,2,0,1:T(8,128)} %copy.31), calls=%async_computation.5 | async-start | bytes 1048576 | tf_op jit(solution)/shard_map/all_to_all | solution.py:46
  143.1 341.7 %all-reduce.11.cloned.1.call-start = ((), (), s32[]{:S(2)}) async-start(), calls=%async_computation.14 | async-start | bytes 1048576 | tf_op jit(solution)/shard_map/psum | solution.py:26
  159.0 30.2 %collective-permute-start.2 = (f32[2,256,256]{2,1,0:T(8,128)}, f32[2,256,256]{2,1,0:T(8,128)}, u32[]{:S(2)}, u32[]{:S(2)}) collective-permute-start(f32[2,256,256]{2,1,0:T(8,128)} %collective-permute-done.1), channel_id=1, source_target_pairs={{0,4},{1,5},{2,6},{3,7},{4,0},{5,1},{6,2},{7,3},{8,12},{9,13},{10,... | collective-permute-start | bytes 1572872 | tf_op jit(solution)/shard_map/ppermute | solution.py:15
  189.3 23.4 %collective-permute-start.3 = (f32[2,256,256]{2,1,0:T(8,128)}, f32[2,256,256]{2,1,0:T(8,128)}, u32[]{:S(2)}, u32[]{:S(2)}) collective-permute-start(f32[2,256,256]{2,1,0:T(8,128)} %collective-permute-done.2), channel_id=1, source_target_pairs={{0,8},{1,9},{2,10},{3,11},{4,12},{5,13},{6,14},{7,15},{8,0},{9,1},... | collective-permute-start | bytes 1572872 | tf_op jit(solution)/shard_map/ppermute | solution.py:15
  196.1 3.3 copy-start.1
  537.5 24.0 %all-to-all-start.8 = ((f32[2,16,16,256]{3,2,0,1:T(8,128)}), f32[2,16,16,256]{3,2,0,1:T(8,128)S(1)}, u32[]{:S(2)}, u32[]{:S(2)}) async-start(f32[2,16,16,256]{3,2,0,1:T(8,128)} %copy.36), calls=%async_computation.8 | async-start | bytes 1048576 | tf_op jit(solution)/shard_map/all_to_all | solution.py:46
  542.4 307.6 %all-reduce.9.cloned.1.call-start = ((), (), s32[]{:S(2)}) async-start(), calls=%async_computation.13 | async-start | bytes 1048576 | tf_op jit(solution)/shard_map/psum | solution.py:26
  543.8 33.4 %collective-permute-start.4 = (f32[2,256,256]{2,1,0:T(8,128)}, f32[2,256,256]{2,1,0:T(8,128)}, u32[]{:S(2)}, u32[]{:S(2)}) collective-permute-start(f32[2,256,256]{2,1,0:T(8,128)} %collective-permute-done.3), channel_id=1, source_target_pairs={{1,0},{2,1},{3,2},{4,3},{5,4},{6,5},{7,6},{8,7},{9,8},{10,9},{11,1... | collective-permute-start | bytes 1572872 | tf_op jit(solution)/shard_map/ppermute | solution.py:21
  561.7 1.7 copy-start.2
  902.8 24.0 %all-to-all-start.11 = ((f32[2,16,16,256]{3,2,0,1:T(8,128)}), f32[2,16,16,256]{3,2,0,1:T(8,128)S(1)}, u32[]{:S(2)}, u32[]{:S(2)}) async-start(f32[2,16,16,256]{3,2,0,1:T(8,128)} %copy.41), calls=%async_computation.11 | async-start | bytes 1048576 | tf_op jit(solution)/shard_map/all_to_all | solution.py:46
  907.6 304.3 %all-reduce.7.cloned.1.call-start = ((), (), s32[]{:S(2)}) async-start(), calls=%async_computation.12 | async-start | bytes 1048576 | tf_op jit(solution)/shard_map/psum | solution.py:26
  909.0 35.8 %collective-permute-start.5 = (f32[2,256,256]{2,1,0:T(8,128)}, f32[2,256,256]{2,1,0:T(8,128)S(1)}, u32[]{:S(2)}, u32[]{:S(2)}) collective-permute-start(f32[2,256,256]{2,1,0:T(8,128)} %collective-permute-done.3), channel_id=1, source_target_pairs={{2,0},{3,1},{4,2},{5,3},{6,4},{7,5},{8,6},{9,7},{10,8},{11,9},{12,... | collective-permute-start | bytes 1572872 | tf_op jit(solution)/shard_map/ppermute | solution.py:21
  926.9 1.7 copy-start.3
Sparse Core Ops, SparseCore 0:
  200.8 283.9 all-reduce.10
  568.1 281.8 all-reduce.8
  933.3 278.5 all-reduce.6
where the time goes:
time: 1220 us
  waiting for transfers between devices  948 us (78%)
  blocking collectives  134 us (11%)
  starting transfers between devices  77.8 us (6%)
  matrix products  26.2 us (2%)
  between operations  17.7 us (1%)
  local copies, waits for them, and re-layouts  14.9 us (1%)
    psum x3, waiting for transfers between devices, spread(): return lax.psum(kept, axis)  807 us
    all_to_all x3, blocking collectives, across_cols(): lax.all_to_all(pieces, 'col', split_axis=1, concat_axis=1, tiled=True)  86.2 us
    all_to_all x2, blocking collectives, mirrored(): lax.all_to_all(by_target, 'row', split_axis=0, concat_axis=0, tiled=True)  47.8 us
    ppermute x4, waiting for transfers between devices, swapped(): return lax.ppermute(value, axis, pairs)  47.4 us
    all_to_all x5, waiting for transfers between devices, across_cols(): lax.all_to_all(pieces, 'col', split_axis=1, concat_axis=1, tiled=True)  44.9 us
    all_to_all x2, waiting for transfers between devices, mirrored(): lax.all_to_all(by_target, 'row', split_axis=0, concat_axis=0, tiled=True)  28 us
    all_to_all x5, starting transfers between devices, across_cols(): lax.all_to_all(pieces, 'col', split_axis=1, concat_axis=1, tiled=True)  25.6 us
  transfers between devices with their start and end apart: 16, of which 14 were waited for; matrix products, arithmetic and copies ran while one was open for 3% of the time, Pallas kernels for 0%

commit v1 on v0

--- a/solution.py
+++ b/solution.py
@@ -2,6 +2,7 @@
 import jax.numpy as jnp
 from jax import lax
 from jax.sharding import PartitionSpec as P
+from jax.lax import all_to_all, axis_size
 
 FRONTS = 3
 DOUBLINGS = 5
@@ -43,7 +44,16 @@
 
 
 def across_cols(pieces):
-    return lax.all_to_all(pieces, "col", split_axis=1, concat_axis=1, tiled=True)
+
+    def run_rates_up(vec):
+        left_arr = axis_size("col")
+        everything = jnp.split(vec, left_arr, 1)
+        val2 = jnp.stack(everything, 0)
+        block_now = all_to_all(val2, "col", split_axis=0, concat_axis=0)
+        z = jnp.concatenate(block_now, 1)
+        return z
+
+    return run_rates_up(pieces)
 
 
 def mirrored(tile_set):

time: 1220 us -> 1250 us (1.025)
  local copies, waits for them, and re-layouts: 14.9 us -> 74.2 us
  blocking collectives: 134 us -> 100 us
  waiting for transfers between devices: 948 us -> 922 us
  starting transfers between devices: 77.8 us -> 103 us
    unnamed x12 -> x134, local copies, waits for them, and re-layouts: 0.24 us -> 58.6 us
    all_to_all x3 -> x2, blocking collectives: 86.2 us -> 53.3 us  [run_rates_up(): block_now = all_to_all(val2, 'col', split_axis=0, concat_axis=0)]
    all_to_all x2, waiting for transfers between devices: 28 us -> 6.73 us  [mirrored(): lax.all_to_all(by_target, 'row', split_axis=0, concat_axis=0, tiled=True)]
    all_to_all x5 -> x6, starting transfers between devices: 25.6 us -> 43.1 us  [run_rates_up(): block_now = all_to_all(val2, 'col', split_axis=0, concat_axis=0)]
    all_to_all x5 -> x6, waiting for transfers between devices: 44.9 us -> 46.1 us  [run_rates_up(): block_now = all_to_all(val2, 'col', split_axis=0, concat_axis=0)]
  transfers between devices with their start and end apart: 16 -> 17, of which waited for: 14 -> 14; matrix products, arithmetic and copies ran while one was open for 3% -> 5% of each run, Pallas kernels for 0% -> 0%
where the time goes in v1:
time: 1250 us
  waiting for transfers between devices  922 us (74%)
  starting transfers between devices  103 us (8%)
  blocking collectives  100 us (8%)
  local copies, waits for them, and re-layouts  74.2 us (6%)
  matrix products  27.1 us (2%)
  between operations  18.1 us (1%)
    psum x3, waiting for transfers between devices, spread(): return lax.psum(kept, axis)  808 us
    unnamed x134, local copies, waits for them, and re-layouts  58.6 us
    all_to_all x2, blocking collectives, run_rates_up(): block_now = all_to_all(val2, 'col', split_axis=0, concat_axis=0)  53.3 us
    all_to_all x2, blocking collectives, mirrored(): lax.all_to_all(by_target, 'row', split_axis=0, concat_axis=0, tiled=True)  47 us
    all_to_all x6, waiting for transfers between devices, run_rates_up(): block_now = all_to_all(val2, 'col', split_axis=0, concat_axis=0)  46.1 us
    all_to_all x6, starting transfers between devices, run_rates_up(): block_now = all_to_all(val2, 'col', split_axis=0, concat_axis=0)  43.1 us
    ppermute x4, waiting for transfers between devices, swapped(): return lax.ppermute(value, axis, pairs)  40.6 us
  transfers between devices with their start and end apart: 17, of which 14 were waited for; matrix products, arithmetic and copies ran while one was open for 5% of the time, Pallas kernels for 0%

profile of v1, /device:TPU:1, one launch (start us, length us, event | category | flops | bytes accessed | tf_op | source)
XLA Modules:
  0.0 1247.8 jit_solution(11327798257530110574)
XLA Ops:
  6.5 1.0 slice_bitcast_fusion.112
  11.7 0.6 constant_dynamic-update-slice_fusion.40
  17.2 16.3 %all-to-all-start.3 = ((f32[16,2,1,16,256]{4,3,1,2,0:T(8,128)}), f32[16,2,1,16,256]{4,3,1,2,0:T(8,128)S(1)}, u32[]{:S(2)}, u32[]{:S(2)}) async-start(f32[16,2,1,16,256]{4,3,1,2,0:T(8,128)} %constant_dynamic-update-slice_fusion.32), calls=%async_computation.3 | async-start | bytes 1048576 | tf_op jit(solution)/shard_map/all_to_all | solution.py:52
  33.5 1.4 constant_dynamic-update-slice_fusion.15
  34.9 1.4 constant_dynamic-update-slice_fusion.14
  36.3 1.4 constant_dynamic-update-slice_fusion.13
  37.7 1.4 constant_dynamic-update-slice_fusion.12
  39.0 0.6 constant_dynamic-update-slice_fusion.11
  41.5 0.6 constant_dynamic-update-slice_fusion.7
  46.4 5.2 all-to-all-done.3
  51.6 6.3 all-to-all-start
  57.9 0.8 copy.487
  58.8 16.2 %all-to-all-done = f32[16,2,1,16,256]{4,3,1,2,0:T(8,128)S(1)} async-done(((f32[16,2,1,16,256]{4,3,1,2,0:T(8,128)}), f32[16,2,1,16,256]{4,3,1,2,0:T(8,128)S(1)}, u32[]{:S(2)}, u32[]{:S(2)}) %all-to-all-start) | async-done | bytes 524320 | tf_op jit(solution)/shard_map/all_to_all | solution.py:52
  74.9 10.1 all-to-all-start.4
  85.1 3.5 collective-permute-start
  89.4 11.3 collective-permute-done
  100.7 3.1 collective-permute-start.1
  103.8 0.8 copy.469
  104.6 8.7 all-to-all-start.1
  123.0 6.7 all-to-all-done.1
  129.7 5.4 all-to-all-start.5
  135.2 0.6 constant_dynamic-update-slice_fusion.31
  138.3 0.6 constant_dynamic-update-slice_fusion.26
  142.6 0.6 constant_dynamic-update-slice_fusion.19
  145.1 9.2 all-to-all-done.5
  154.3 5.3 all-to-all-start.2
  160.3 7.1 collective-permute-start.2
  169.5 23.9 %collective-permute-done.2 = f32[2,256,256]{2,1,0:T(8,128)} collective-permute-done((f32[2,256,256]{2,1,0:T(8,128)}, f32[2,256,256]{2,1,0:T(8,128)}, u32[]{:S(2)}, u32[]{:S(2)}) %collective-permute-start.2) | collective-permute-done | bytes 524320 | tf_op jit(solution)/shard_map/ppermute | solution.py:16
  193.4 7.3 collective-permute-start.3
  200.7 0.8 copy.504
  201.6 1.1 copy.485
  202.8 0.8 copy.486
  203.6 1.5 fusion.20
  205.2 0.7 bitcast_dynamic-update-slice_fusion.2
  207.0 0.7 bitcast_dynamic-update-slice_fusion.1
  207.6 0.7 bitcast_dynamic-update-slice_fusion
  208.3 0.6 fusion.4
  212.7 0.8 select_bitcast_fusion.5
  213.6 5.5 collective-permute-done.3
  219.1 2.4 gather_fusion
  221.5 271.6 %all-reduce.11.cloned.1.call-done = (f32[1,256,256]{2,1,0:T(8,128)}, f32[1,256,256]{2,1,0:T(8,128)}) async-done(((f32[1,256,256]{2,1,0:T(8,128)}, f32[1,256,256]{2,1,0:T(8,128)}), (f32[1,256,256]{2,1,0:T(8,128)}, f32[1,256,256]{2,1,0:T(8,128)})) %all-reduce.11.cloned.1.call-update) | async-done | bytes 524304 | tf_op jit(solution)/shard_map/psum | solution.py:27
  493.0 1.9 fusion.3
  495.1 26.7 %all_to_all.60 = f32[16,2,1,16,256]{4,3,1,2,0:T(8,128)S(1)} all-to-all(f32[16,2,1,16,256]{4,3,1,2,0:T(8,128)S(1)} %constant_dynamic-update-slice_fusion.65), channel_id=1, replica_groups=mesh['row'=32,'col'=16] {'col'}, dimensions={0} | all-to-all | bytes 1048576 | tf_op jit(solution)/shard_map/all_to_all | solution.py:52
  521.8 23.5 %all_to_all.61 = f32[32,16,256]{2,1,0:T(8,128)S(1)} all-to-all(f32[32,16,256]{2,1,0:T(8,128)S(1)} %bitcast.1038), channel_id=1, replica_groups=mesh['row'=32,'col'=16] {'row'}, dimensions={0} | all-to-all | bytes 1048576 | tf_op jit(solution)/shard_map/all_to_all | solution.py:66
  545.3 0.6 constant_dynamic-update-slice_fusion.96
  549.6 0.6 constant_dynamic-update-slice_fusion.89
  555.2 4.9 all-to-all-start.8
  561.4 9.5 collective-permute-start.4
  571.0 8.2 all-to-all-done.8
  584.8 0.8 select_bitcast_fusion.3
  585.7 9.1 collective-permute-done.4
  594.8 2.4 gather_fusion.1
  597.2 270.2 %all-reduce.9.cloned.1.call-done = (f32[1,256,256]{2,1,0:T(8,128)}, f32[1,256,256]{2,1,0:T(8,128)}) async-done(((f32[1,256,256]{2,1,0:T(8,128)}, f32[1,256,256]{2,1,0:T(8,128)}), (f32[1,256,256]{2,1,0:T(8,128)}, f32[1,256,256]{2,1,0:T(8,128)})) %all-reduce.9.cloned.1.call-update) | async-done | bytes 524304 | tf_op jit(solution)/shard_map/psum | solution.py:27
  867.4 1.9 fusion.2
  869.5 26.7 %all_to_all.62 = f32[16,2,1,16,256]{4,3,1,2,0:T(8,128)S(1)} all-to-all(f32[16,2,1,16,256]{4,3,1,2,0:T(8,128)S(1)} %constant_dynamic-update-slice_fusion.97), channel_id=1, replica_groups=mesh['row'=32,'col'=16] {'col'}, dimensions={0} | all-to-all | bytes 1048576 | tf_op jit(solution)/shard_map/all_to_all | solution.py:52
  896.2 23.5 %all_to_all.63 = f32[32,16,256]{2,1,0:T(8,128)S(1)} all-to-all(f32[32,16,256]{2,1,0:T(8,128)S(1)} %bitcast.1039), channel_id=1, replica_groups=mesh['row'=32,'col'=16] {'row'}, dimensions={0} | all-to-all | bytes 1048576 | tf_op jit(solution)/shard_map/all_to_all | solution.py:66
  919.7 0.6 constant_dynamic-update-slice_fusion.128
  929.6 4.9 all-to-all-start.11
  935.8 10.5 collective-permute-start.5
  946.2 7.3 all-to-all-done.11
  959.2 0.8 select_bitcast_fusion.1
  960.1 11.4 collective-permute-done.5
  972.1 266.6 %all-reduce.7.cloned.1.call-done = (f32[1,256,256]{2,1,0:T(8,128)}, f32[1,256,256]{2,1,0:T(8,128)}) async-done(((f32[1,256,256]{2,1,0:T(8,128)}, f32[1,256,256]{2,1,0:T(8,128)}), (f32[1,256,256]{2,1,0:T(8,128)}, f32[1,256,256]{2,1,0:T(8,128)})) %all-reduce.7.cloned.1.call-update) | async-done | bytes 524304 | tf_op jit(solution)/shard_map/psum | solution.py:27
  1238.7 2.5 fusion.1
  (204 shorter events, 69.9 us)
Async XLA Ops:
  6.5 32.5 %copy-start.4 = (f32[1,2,1,256,256]{4,3,2,1,0:T(8,128)S(1)}, f32[1,2,1,256,256]{4,3,2,1,0:T(8,128)}, u32[]{:S(2)}) copy-start(f32[1,2,1,256,256]{4,3,2,1,0:T(8,128)} %param.5) | copy-start | bytes 1572868
  17.2 67.9 %copy-start.6 = (f32[1,2,1,256,256]{4,3,2,1,0:T(8,128)S(1)}, f32[1,2,1,256,256]{4,3,2,1,0:T(8,128)}, u32[]{:S(2)}) copy-start(f32[1,2,1,256,256]{4,3,2,1,0:T(8,128)} %param.6) | copy-start | bytes 1572868
  17.2 71.4 %copy-start = (f32[1,256,256]{2,1,0:T(8,128)S(1)}, f32[1,256,256]{2,1,0:T(8,128)}, u32[]{:S(2)}) copy-start(f32[1,256,256]{2,1,0:T(8,128)} %param.7) | copy-start | bytes 786436
  17.2 34.4 %all-to-all-start.3 = ((f32[16,2,1,16,256]{4,3,1,2,0:T(8,128)}), f32[16,2,1,16,256]{4,3,1,2,0:T(8,128)S(1)}, u32[]{:S(2)}, u32[]{:S(2)}) async-start(f32[16,2,1,16,256]{4,3,1,2,0:T(8,128)} %constant_dynamic-update-slice_fusion.32), calls=%async_computation.3 | async-start | bytes 1048576 | tf_op jit(solution)/shard_map/all_to_all | solution.py:52
  51.6 23.3 %all-to-all-start = ((f32[16,2,1,16,256]{4,3,1,2,0:T(8,128)}), f32[16,2,1,16,256]{4,3,1,2,0:T(8,128)S(1)}, u32[]{:S(2)}, u32[]{:S(2)}) async-start(f32[16,2,1,16,256]{4,3,1,2,0:T(8,128)} %constant_dynamic-update-slice_fusion), calls=%async_computation | async-start | bytes 1048576 | tf_op jit(solution)/shard_map/all_to_all | solution.py:52
  74.9 29.7 %all-to-all-start.4 = ((f32[32,16,256]{2,1,0:T(8,128)}), f32[32,16,256]{2,1,0:T(8,128)S(1)}, u32[]{:S(2)}, u32[]{:S(2)}) async-start(f32[32,16,256]{2,1,0:T(8,128)} %bitcast.62), calls=%async_computation.4 | async-start | bytes 1048576 | tf_op jit(solution)/shard_map/all_to_all | solution.py:66
  85.1 15.6 %collective-permute-start = (f32[2,256,256]{2,1,0:T(8,128)S(1)}, f32[2,256,256]{2,1,0:T(8,128)}, u32[]{:S(2)}, u32[]{:S(2)}) collective-permute-start(f32[2,256,256]{2,1,0:T(8,128)S(1)} %bitcast.1043), channel_id=1, source_target_pairs={{0,1},{1,0},{2,3},{3,2},{4,5},{5,4},{6,7},{7,6},{8,9},{9,8},{10,11... | collective-permute-start | bytes 1572872 | tf_op jit(solution)/shard_map/ppermute | solution.py:16
  100.7 59.6 %collective-permute-start.1 = (f32[2,256,256]{2,1,0:T(8,128)}, f32[2,256,256]{2,1,0:T(8,128)}, u32[]{:S(2)}, u32[]{:S(2)}) collective-permute-start(f32[2,256,256]{2,1,0:T(8,128)} %collective-permute-done), channel_id=1, source_target_pairs={{0,2},{1,3},{2,0},{3,1},{4,6},{5,7},{6,4},{7,5},{8,10},{9,11},{10,... | collective-permute-start | bytes 1572872 | tf_op jit(solution)/shard_map/ppermute | solution.py:16
  104.6 25.1 %all-to-all-start.1 = ((f32[32,16,256]{2,1,0:T(8,128)}), f32[32,16,256]{2,1,0:T(8,128)S(1)}, u32[]{:S(2)}, u32[]{:S(2)}) async-start(f32[32,16,256]{2,1,0:T(8,128)} %bitcast.22), calls=%async_computation.1 | async-start | bytes 1048576 | tf_op jit(solution)/shard_map/all_to_all | solution.py:66
  129.7 24.6 %all-to-all-start.5 = ((f32[16,2,1,16,256]{4,3,1,2,0:T(8,128)}), f32[16,2,1,16,256]{4,3,1,2,0:T(8,128)S(1)}, u32[]{:S(2)}, u32[]{:S(2)}) async-start(f32[16,2,1,16,256]{4,3,1,2,0:T(8,128)} %constant_dynamic-update-slice_fusion.48), calls=%async_computation.5 | async-start | bytes 1048576 | tf_op jit(solution)/shard_map/all_to_all | solution.py:52
  154.3 47.3 %all-to-all-start.2 = ((f32[16,2,1,16,256]{4,3,1,2,0:T(8,128)}), f32[16,2,1,16,256]{4,3,1,2,0:T(8,128)}, u32[]{:S(2)}, u32[]{:S(2)}) async-start(f32[16,2,1,16,256]{4,3,1,2,0:T(8,128)} %constant_dynamic-update-slice_fusion.16), calls=%async_computation.2 | async-start | bytes 1048576 | tf_op jit(solution)/shard_map/all_to_all | solution.py:52
  159.6 333.4 %all-reduce.11.cloned.1.call-start = ((), (), s32[]{:S(2)}) async-start(), calls=%async_computation.14 | async-start | bytes 1048576 | tf_op jit(solution)/shard_map/psum | solution.py:27
  160.3 33.1 %collective-permute-start.2 = (f32[2,256,256]{2,1,0:T(8,128)}, f32[2,256,256]{2,1,0:T(8,128)}, u32[]{:S(2)}, u32[]{:S(2)}) collective-permute-start(f32[2,256,256]{2,1,0:T(8,128)} %collective-permute-done.1), channel_id=1, source_target_pairs={{0,4},{1,5},{2,6},{3,7},{4,0},{5,1},{6,2},{7,3},{8,12},{9,13},{10,... | collective-permute-start | bytes 1572872 | tf_op jit(solution)/shard_map/ppermute | solution.py:16
  193.4 25.7 %collective-permute-start.3 = (f32[2,256,256]{2,1,0:T(8,128)}, f32[2,256,256]{2,1,0:T(8,128)}, u32[]{:S(2)}, u32[]{:S(2)}) collective-permute-start(f32[2,256,256]{2,1,0:T(8,128)} %collective-permute-done.2), channel_id=1, source_target_pairs={{0,8},{1,9},{2,10},{3,11},{4,12},{5,13},{6,14},{7,15},{8,0},{9,1},... | collective-permute-start | bytes 1572872 | tf_op jit(solution)/shard_map/ppermute | solution.py:16
  201.6 3.6 copy-start.5
  209.0 3.3 copy-start.1
  555.2 24.0 %all-to-all-start.8 = ((f32[16,2,1,16,256]{4,3,1,2,0:T(8,128)}), f32[16,2,1,16,256]{4,3,1,2,0:T(8,128)S(1)}, u32[]{:S(2)}, u32[]{:S(2)}) async-start(f32[16,2,1,16,256]{4,3,1,2,0:T(8,128)} %constant_dynamic-update-slice_fusion.81), calls=%async_computation.8 | async-start | bytes 1048576 | tf_op jit(solution)/shard_map/all_to_all | solution.py:52
  560.1 307.3 %all-reduce.9.cloned.1.call-start = ((), (), s32[]{:S(2)}) async-start(), calls=%async_computation.13 | async-start | bytes 1048576 | tf_op jit(solution)/shard_map/psum | solution.py:27
  561.4 33.4 %collective-permute-start.4 = (f32[2,256,256]{2,1,0:T(8,128)}, f32[2,256,256]{2,1,0:T(8,128)}, u32[]{:S(2)}, u32[]{:S(2)}) collective-permute-start(f32[2,256,256]{2,1,0:T(8,128)} %collective-permute-done.3), channel_id=1, source_target_pairs={{1,0},{2,1},{3,2},{4,3},{5,4},{6,5},{7,6},{8,7},{9,8},{10,9},{11,1... | collective-permute-start | bytes 1572872 | tf_op jit(solution)/shard_map/ppermute | solution.py:22
  579.4 1.7 copy-start.2
  929.6 24.0 %all-to-all-start.11 = ((f32[16,2,1,16,256]{4,3,1,2,0:T(8,128)}), f32[16,2,1,16,256]{4,3,1,2,0:T(8,128)S(1)}, u32[]{:S(2)}, u32[]{:S(2)}) async-start(f32[16,2,1,16,256]{4,3,1,2,0:T(8,128)} %constant_dynamic-update-slice_fusion.113), calls=%async_computation.11 | async-start | bytes 1048576 | tf_op jit(solution)/shard_map/all_to_all | solution.py:52
  934.4 304.3 %all-reduce.7.cloned.1.call-start = ((), (), s32[]{:S(2)}) async-start(), calls=%async_computation.12 | async-start | bytes 1048576 | tf_op jit(solution)/shard_map/psum | solution.py:27
  935.8 35.7 %collective-permute-start.5 = (f32[2,256,256]{2,1,0:T(8,128)}, f32[2,256,256]{2,1,0:T(8,128)S(1)}, u32[]{:S(2)}, u32[]{:S(2)}) collective-permute-start(f32[2,256,256]{2,1,0:T(8,128)} %collective-permute-done.3), channel_id=1, source_target_pairs={{2,0},{3,1},{4,2},{5,3},{6,4},{7,5},{8,6},{9,7},{10,8},{11,9},{12,... | collective-permute-start | bytes 1572872 | tf_op jit(solution)/shard_map/ppermute | solution.py:22
  953.7 1.7 copy-start.3
Sparse Core Ops, SparseCore 0:
  213.7 279.3 all-reduce.10
  585.8 281.5 all-reduce.8
  960.2 278.5 all-reduce.6
